TPU v7x, 32 devices: a whole 2x2x4 slice. The times are simulated.
32 devices in a mesh: space: 4 (over y, core), tm: 8 (over z, x).
Axes of the slice: x: 2, y: 2, z: 4, core: 2. Of those that a mesh axis runs over, the one named last changes fastest.
Arguments:
- snapshots: float32 [2048, 30720], P('tm', 'space'), may hold values from -6 to 6
- closing: float32 [128, 30720], P(None, 'space'), may hold values from -6 to 6
- weights: float32 [30720], P('space'), may hold values from 0.25 to 36, as said below
- bin_index: int32 [64], replicated, may hold values from 0 to 128, as said below
Outputs:
- spectra: float32 [64, 2, 16, 16], P('tm', None, 'space')
Inputs may be any that keep to these rules, and one draw needn't show every extreme that they name: `bin_index`: distinct bins. Positive weights.
All inputs are finite; a program needn't handle non-finite values.
Results may differ from a plain program's by a relative error of at most 0.0003.
Values sent between devices are 32-bit elements; how exact they have to be, the bound alone decides.
A program may use at most 128 MiB of HBM per device.

v0:
```python
import functools

import jax
import jax.numpy as jnp
import numpy as np
from jax import lax
from jax.experimental import pallas as pl
from jax.experimental.pallas import tpu as pltpu
from jax.sharding import PartitionSpec as P

NFFT = 256
NBINS = 64
LANES = 128
MESH = pl.DeviceIdType.MESH


def passed_along(array, axis, by):
    peers = lax.axis_size(axis)
    pairs = [(i, i + by) for i in range(peers) if 0 <= i + by < peers]
    return lax.ppermute(array, axis, pairs)


def spectral_table(bin_index, length):
    sample = jnp.arange(length, dtype=jnp.int32)
    window = 0.5 - 0.5 * jnp.cos(2.0 * jnp.pi * sample.astype(jnp.float32) / length)
    phase_turns = sample[:, None] * bin_index[None, :] % length
    phase_angle = 2.0 * jnp.pi * phase_turns.astype(jnp.float32) / length
    paired = jnp.stack(
        [window[:, None] * jnp.cos(phase_angle), -window[:, None] * jnp.sin(phase_angle)], axis=2
    )
    return paired.reshape(length, 2 * bin_index.shape[0])


def cross_spectra(first_set, second_set):
    products = jnp.einsum(
        "kaip,kbjp->kabij", first_set, second_set, precision=lax.Precision.HIGHEST
    )
    real_part = products[:, 0, 0] + products[:, 1, 1]
    imag_part = products[:, 0, 1] - products[:, 1, 0]
    return jnp.stack([real_part, imag_part], axis=1)


def body(snapshots, closing, weights, bin_index):
    stride_rows = NFFT // 2
    tail_rows = closing.shape[0]
    blocks_here = snapshots.shape[0] // stride_rows
    points = snapshots.shape[1]
    width_tm = lax.axis_size("tm")
    width_space = lax.axis_size("space")
    blocks_all = blocks_here * width_tm
    own_rows = blocks_all // width_space
    basis_table = spectral_table(bin_index, NFFT)
    incoming = passed_along(snapshots[:tail_rows], "tm", -1)
    last_device = lax.axis_index("tm") == width_tm - 1
    series = jnp.concatenate([snapshots, jnp.where(last_device, closing, incoming)], axis=0)
    leading = series[: blocks_here * stride_rows].reshape(blocks_here, stride_rows, points)
    trailing = series[stride_rows:].reshape(blocks_here, stride_rows, points)
    pieces = jnp.concatenate([leading, trailing], axis=1)
    spectrum = jnp.einsum("nc,bnp->cbp", basis_table, pieces, precision=lax.Precision.HIGHEST)
    spectrum = spectrum.reshape(NBINS, 2, blocks_here, points)
    gathered = lax.all_to_all(spectrum, "tm", split_axis=0, concat_axis=2, tiled=True)
    weighted = gathered * weights
    summed = lax.psum_scatter(
        cross_spectra(gathered, weighted).transpose(2, 0, 1, 3),
        "space",
        scatter_dimension=0,
        tiled=True,
    )
    row_ids = lax.axis_index("space") * own_rows + jnp.arange(own_rows, dtype=jnp.int32)
    diagonal = (row_ids[:, None] == jnp.arange(blocks_all, dtype=jnp.int32)[None, :]).astype(
        jnp.float32
    )
    local_trace = jnp.einsum(
        "rkj,rj->k", summed[:, :, 0, :], diagonal, precision=lax.Precision.HIGHEST
    )
    energy = lax.psum(local_trace, "space")
    spectra = summed * (blocks_all / energy)[None, :, None, None]
    return spectra.transpose(1, 2, 0, 3)


def tile_start(device, tiles, width_tm, space):
    return (device * tiles + (space % 2) * (width_tm // 2)) // width_tm


def halves(value):
    high = value.astype(jnp.bfloat16)
    return high, (value - high.astype(jnp.float32)).astype(jnp.bfloat16)


def matmul(a, b):
    return lax.dot_general(a, b, (((1,), (0,)), ((), ())), preferred_element_type=jnp.float32)


def matmul_nt(a, b):
    return lax.dot_general(a, b, (((1,), (1,)), ((), ())), preferred_element_type=jnp.float32)


def exact(a, b):
    return jnp.dot(a, b, precision=lax.Precision.HIGHEST, preferred_element_type=jnp.float32)


def picked(selector, values):
    high, low = halves(values)
    return matmul(selector, high) + matmul(selector, low)


def picked_right(values, selector):
    high, low = halves(values)
    return matmul(high, selector) + matmul(low, selector)


def table_rows(bins, length):
    shape = (bins.shape[0], length)
    sample = lax.broadcasted_iota(jnp.int32, shape, 1)
    odd = (lax.broadcasted_iota(jnp.int32, shape, 0) & 1) == 1
    window = 0.5 - 0.5 * jnp.cos(2.0 * jnp.pi * sample.astype(jnp.float32) / length)
    turns = (sample * bins) & (length - 1)
    angle = 2.0 * jnp.pi * turns.astype(jnp.float32) / length
    return window * jnp.where(odd, -jnp.sin(angle), jnp.cos(angle))


def kernel(
    n,
    n_space,
    snap_ref,
    closing_ref,
    weights_ref,
    bins_ref,
    left_ref,
    even_ref,
    odd_ref,
    ones_ref,
    out_ref,
    series,
    table_ref,
    a_high,
    a_low,
    b_high,
    b_low,
    gram,
    part,
    rows_in,
    mine,
    spread,
    local_sem,
    send_sem,
    recv_sem,
    part_send,
    part_recv,
    space_send,
    space_recv,
):
    me = lax.axis_index("tm")
    here = lax.axis_index("space")
    rows, points = snap_ref.shape
    tail_rows = closing_ref.shape[0]
    tiles = points // LANES
    slots = series.shape[0]
    hop = NFFT // 2
    blocks_all = n * rows // hop
    channels = bins_ref.shape[0]
    group = channels // n

    near = me // (n // 2) * (n // 2)
    far = n // 2 - near

    def peer_of(k):
        return lax.rem(me + k, n)

    def near_peer(k):
        return near + lax.rem(me - near + k, n // 2)

    def far_peer(k):
        return far + lax.rem(me - near + k, n // 2)

    peers_near = [near_peer(k) for k in range(1, n // 2)]
    peers_far = [far_peer(k) for k in range(n // 2)]

    def begin(device):
        return tile_start(device, tiles, n, here)

    def count(device):
        return begin(device + 1) - begin(device)

    my_start, my_count = begin(me), count(me)

    def columns(tile):
        return pl.ds(pl.multiple_of(tile * LANES, LANES), LANES)

    def own_copies(t):
        return (
            pltpu.make_async_copy(
                snap_ref.at[:, columns(my_start + t)],
                series.at[t, pl.ds(pl.multiple_of(me * rows, rows), rows)],
                local_sem.at[0, t],
            ),
            pltpu.make_async_copy(
                closing_ref.at[:, columns(my_start + t)],
                series.at[t, pl.ds(n * rows, tail_rows)],
                local_sem.at[1, t],
            ),
        )

    def outgoing(t, peer):
        return pltpu.make_async_remote_copy(
            src_ref=snap_ref.at[:, columns(begin(peer) + t)],
            dst_ref=series.at[t, pl.ds(pl.multiple_of(me * rows, rows), rows)],
            send_sem=send_sem.at[t, peer],
            recv_sem=recv_sem.at[t, me],
            device_id={"tm": peer},
            device_id_type=MESH,
        )

    def incoming(t, peer):
        return pltpu.make_async_remote_copy(
            src_ref=snap_ref.at[:, columns(my_start + t)],
            dst_ref=series.at[t, pl.ds(pl.multiple_of(peer * rows, rows), rows)],
            send_sem=send_sem.at[t, peer],
            recv_sem=recv_sem.at[t, peer],
            device_id={"tm": peer},
            device_id_type=MESH,
        )

    barrier = pltpu.get_barrier_semaphore()
    for k in range(1, n):
        pl.semaphore_signal(barrier, inc=1, device_id={"tm": peer_of(k)}, device_id_type=MESH)
    for k in range(1, n_space):
        pl.semaphore_signal(
            barrier, inc=1, device_id={"space": lax.rem(here + k, n_space)}, device_id_type=MESH
        )
    pl.semaphore_wait(barrier, n - 1 + n_space - 1)

    @pl.loop(0, slots)
    def _(t):
        for peer in [peer_of(k) for k in range(1, n)]:

            @pl.when(t < count(peer))
            def _(peer=peer):
                outgoing(t, peer).start()

        @pl.when(t < my_count)
        def _():
            for copy in own_copies(t):
                copy.start()

    @pl.when(my_count < slots)
    def _():
        series[slots - 1] = jnp.zeros(series.shape[1:], jnp.float32)

    gram[...] = jnp.zeros(gram.shape, jnp.float32)
    table_high, table_low = halves(table_rows(bins_ref[...], NFFT))
    table_ref[:channels] = table_high
    table_ref[channels:] = table_low

    @pl.loop(0, slots // 2)
    def _(step):
        def arrived(peers, own):
            for half in range(2):
                t = 2 * step + half

                @pl.when(t < my_count)
                def _(t=t):
                    if own:
                        for copy in own_copies(t):
                            copy.wait()
                    for peer in peers:
                        incoming(t, peer).wait_recv()

        weight = []
        for half in range(2):
            t = 2 * step + half
            held = weights_ref[pl.ds(jnp.minimum(my_start + t, tiles - 1), 1), :]
            weight.append(held * (t < my_count).astype(jnp.float32))
        weight = jnp.concatenate(weight, axis=1)

        def transform(turn, carry):
            block = lax.rem(near * (rows // hop) + turn, blocks_all)
            window = pl.ds(pl.multiple_of(block * hop, hop), NFFT)
            piece = jnp.concatenate(
                [series[2 * step, window, :], series[2 * step + 1, window, :]], axis=1
            )
            high, low = halves(piece)
            both = matmul(table_ref[...], high)
            coef = both[:channels] + both[channels:] + matmul(table_ref[:channels], low)
            first_high, first_low = halves(coef)
            second_high, second_low = halves(coef * weight)
            place = pl.ds(pl.multiple_of(block * group, group), group)
            for g in range(n):
                cut = slice(g * group, (g + 1) * group)
                a_high[g, place, :] = first_high[cut]
                a_low[g, place, :] = first_low[cut]
                b_high[g, place, :] = second_high[cut]
                b_low[g, place, :] = second_low[cut]
            return carry

        ready = blocks_all // 2 - 1
        arrived(peers_near, True)
        lax.fori_loop(0, ready, transform, 0, unroll=ready)
        arrived(peers_far, False)
        lax.fori_loop(ready, blocks_all, transform, 0, unroll=3)

        def products(g, carry):
            gram[g] += (
                matmul_nt(b_high[g], a_high[g])
                + matmul_nt(b_high[g], a_low[g])
                + matmul_nt(b_low[g], a_high[g])
            )
            return carry

        lax.fori_loop(0, n, products, 0, unroll=2)

    size = gram.shape[1]
    row = lax.broadcasted_iota(jnp.int32, (size, size), 0)
    col = lax.broadcasted_iota(jnp.int32, (size, size), 1)
    same_bin = ((row & (group - 1)) >> 1) == ((col & (group - 1)) >> 1)

    def folded(g):
        kept = picked(left_ref[...], jnp.where(same_bin, gram[g], 0.0))
        middle = kept.shape[0] // 2
        return picked_right(kept[:middle], even_ref[...]) + picked_right(
            kept[middle:], odd_ref[...]
        )

    def part_copy(k):
        peer = peer_of(k)
        return pltpu.make_async_remote_copy(
            src_ref=part.at[peer],
            dst_ref=rows_in.at[me],
            send_sem=part_send.at[peer],
            recv_sem=part_recv.at[me],
            device_id={"tm": peer},
            device_id_type=MESH,
        )

    def part_arrival(k):
        peer = peer_of(k)
        return pltpu.make_async_remote_copy(
            src_ref=part.at[peer],
            dst_ref=rows_in.at[peer],
            send_sem=part_send.at[peer],
            recv_sem=part_recv.at[peer],
            device_id={"tm": peer},
            device_id_type=MESH,
        )

    for k in range(1, n):
        part[peer_of(k)] = folded(peer_of(k))
        part_copy(k).start()
    rows_in[me] = folded(me)
    for k in range(1, n):
        part_arrival(k).wait_recv()
    total = rows_in[0]
    for p in range(1, n):
        total = total + rows_in[p]
    mine[...] = total
    spread[here] = total

    def space_copy(k):
        peer = lax.rem(here + k, n_space)
        return pltpu.make_async_remote_copy(
            src_ref=mine,
            dst_ref=spread.at[here],
            send_sem=space_send.at[peer],
            recv_sem=space_recv.at[here],
            device_id={"space": peer},
            device_id_type=MESH,
        )

    def space_arrival(k):
        peer = lax.rem(here + k, n_space)
        return pltpu.make_async_remote_copy(
            src_ref=mine,
            dst_ref=spread.at[peer],
            send_sem=space_send.at[peer],
            recv_sem=space_recv.at[peer],
            device_id={"space": peer},
            device_id_type=MESH,
        )

    for k in range(1, n_space):
        space_copy(k).start()
    for k in range(1, n_space):
        space_arrival(k).wait_recv()
    total = spread[0]
    for p in range(1, n_space):
        total = total + spread[p]
    line = lax.broadcasted_iota(jnp.int32, total.shape, 0)
    lane = lax.broadcasted_iota(jnp.int32, total.shape, 1)
    diagonal = jnp.where(line == (lane & (blocks_all - 1)), total, 0.0)
    trace = jnp.sum(diagonal, axis=0, keepdims=True)
    energy = exact(jnp.broadcast_to(trace, (8, trace.shape[1])), ones_ref[...])[:1]
    out_ref[...] = total * (blocks_all / energy)

    @pl.loop(0, slots)
    def _(t):
        for k in range(1, n):
            peer = peer_of(k)

            @pl.when(t < count(peer))
            def _():
                outgoing(t, peer).wait_send()

    for k in range(1, n):
        part_copy(k).wait_send()
    for k in range(1, n_space):
        space_copy(k).wait_send()


def selections(blocks, group):
    size, bins = blocks * group, group // 2
    block, channel = np.divmod(np.arange(size), group)
    part, second = np.divmod(np.arange(2 * blocks), blocks)
    match = second[:, None] == block[None, :]
    first_half = match & (channel[None, :] % 2 == part[:, None])
    second_half = match & (channel[None, :] % 2 == 1 - part[:, None])
    sign = np.where(part[:, None] == 0, 1.0, -1.0)
    left = np.concatenate([first_half * 1.0, second_half * sign], axis=0)
    bin_of, first = np.divmod(np.arange(bins * blocks), blocks)
    place = (block[:, None] == first[None, :]) & (channel[:, None] // 2 == bin_of[None, :])
    even = place & (channel[:, None] % 2 == 0)
    odd = place & (channel[:, None] % 2 == 1)
    ones = bin_of[:, None] == bin_of[None, :]
    return [jnp.asarray(m, jnp.bfloat16) for m in (left, even, odd)] + [
        jnp.asarray(ones, jnp.float32)
    ]


def fused_body(snapshots, closing, weights, bin_index):
    n, n_space = lax.axis_size("tm"), lax.axis_size("space")
    rows, points = snapshots.shape
    tail_rows = closing.shape[0]
    tiles = points // LANES
    slots = -(-tiles // n)
    blocks_all = n * rows // (NFFT // 2)
    channels = 2 * NBINS
    group = channels // n
    size = blocks_all * group
    shape = (2 * blocks_all, size // 2)
    whole = pl.BlockSpec(memory_space=pltpu.VMEM)
    spread = pl.pallas_call(
        functools.partial(kernel, n, n_space),
        out_shape=jax.ShapeDtypeStruct(shape, jnp.float32),
        in_specs=[pl.BlockSpec(memory_space=pl.ANY)] * 2 + [whole] * 6,
        out_specs=whole,
        scratch_shapes=[
            pltpu.VMEM((slots, n * rows + tail_rows, LANES), jnp.float32),
            pltpu.VMEM((2 * channels, NFFT), jnp.bfloat16),
        ]
        + [pltpu.VMEM((n, size, 2 * LANES), jnp.bfloat16)] * 4
        + [
            pltpu.VMEM((n, size, size), jnp.float32),
            pltpu.VMEM((n,) + shape, jnp.float32),
            pltpu.VMEM((n,) + shape, jnp.float32),
            pltpu.VMEM(shape, jnp.float32),
            pltpu.VMEM((n_space,) + shape, jnp.float32),
            pltpu.SemaphoreType.DMA((2, slots)),
            pltpu.SemaphoreType.DMA((slots, n)),
            pltpu.SemaphoreType.DMA((slots, n)),
            pltpu.SemaphoreType.DMA((n,)),
            pltpu.SemaphoreType.DMA((n,)),
            pltpu.SemaphoreType.DMA((n_space,)),
            pltpu.SemaphoreType.DMA((n_space,)),
        ],
        compiler_params=pltpu.CompilerParams(collective_id=0, has_side_effects=True),
    )(
        snapshots,
        closing,
        weights.reshape(tiles, LANES),
        jnp.repeat(bin_index, 2)[:, None],
        *selections(blocks_all, group),
    )
    by_pair = spread.reshape(2, blocks_all, group // 2, blocks_all).transpose(2, 0, 3, 1)
    own_rows = blocks_all // n_space
    return lax.dynamic_slice_in_dim(by_pair, lax.axis_index("space") * own_rows, own_rows, 2)


def chosen_body(snapshots, closing, weights, bin_index):
    n = lax.axis_size("tm")
    rows, points = snapshots.shape
    group = 2 * NBINS // n
    blocks_all = n * rows // (NFFT // 2)
    slots = -(-(points // LANES) // n)
    fits = (
        2 * NBINS % n == 0
        and n % 2 == 0
        and points % LANES == 0
        and slots % 2 == 0
        and closing.shape[0] == NFFT // 2
        and group == 16
        and blocks_all == 16
    )
    return (fused_body if fits else body)(snapshots, closing, weights, bin_index)


def solution(mesh):
    return jax.shard_map(
        chosen_body,
        mesh=mesh,
        in_specs=(P("tm", "space"), P(None, "space"), P("space"), P()),
        out_specs=P("tm", None, "space", None),
        check_vma=False,
    )
```

profile of v0, /device:TPU:0, one launch (start us, length us, event | category | flops | bytes accessed | tf_op | source)
XLA Modules:
  0.0 194.6 jit_solution(2872004686122116516)
XLA Ops:
  0.0 0.7 broadcast_in_dim.3
  0.7 0.7 broadcast_in_dim_reshape.4.bins_ref
  1.4 191.4 %shard_map.82 = f32[32,128]{1,0:T(8,128)} custom-call(f32[256,7680]{1,0:T(8,128)} %snap_ref.1, f32[128,7680]{1,0:T(8,128)} %closing_ref.1, f32[60,128]{1,0:T(8,128)} %bitcast.2, s32[128,1]{1,0:T(8,128)} %broadcast_in_dim_reshape.4.bins_ref, bf16[64,256]{1,0:T(8,128)(2,1)} %constant.19.clone.left_ref, bf16[256,128]{1,0:T(8,128)(2,1)} %constant.20.clone.even_ref, ...), custom_call_target="tpu_custom_call" | custom-call | tf_op jit(solution)/shard_map/pallas_call | solution.py:440
  192.9 0.8 reshape.7
  193.7 0.1 constant_dynamic-slice_fusion
  193.8 0.8 copy.13
where the time goes:
time: 195 us
  Pallas kernels  191 us (98%)
  local copies, waits for them, and re-layouts  3.12 us (2%)
    pallas_call x1, Pallas kernels, fused_body(): pl.pallas_call(functools.partial(kernel, n, n_space), out_shape=jax.Shape...  191 us

commit v1 on v0

v1 whole, which is shorter than its diff:
```python
import functools

import jax
import jax.numpy as jnp
from jax import lax
from jax.experimental import pallas as pl
from jax.experimental.pallas import tpu as pltpu
from jax.sharding import PartitionSpec as P

NFFT = 256
NBINS = 64
LANES = 128
MESH = pl.DeviceIdType.MESH


def passed_along(array, axis, by):
    peers = lax.axis_size(axis)
    pairs = [(i, i + by) for i in range(peers) if 0 <= i + by < peers]
    return lax.ppermute(array, axis, pairs)


def spectral_table(bin_index, length):
    sample = jnp.arange(length, dtype=jnp.int32)
    window = 0.5 - 0.5 * jnp.cos(2.0 * jnp.pi * sample.astype(jnp.float32) / length)
    phase_turns = sample[:, None] * bin_index[None, :] % length
    phase_angle = 2.0 * jnp.pi * phase_turns.astype(jnp.float32) / length
    paired = jnp.stack(
        [window[:, None] * jnp.cos(phase_angle), -window[:, None] * jnp.sin(phase_angle)], axis=2
    )
    return paired.reshape(length, 2 * bin_index.shape[0])


def cross_spectra(first_set, second_set):
    products = jnp.einsum(
        "kaip,kbjp->kabij", first_set, second_set, precision=lax.Precision.HIGHEST
    )
    real_part = products[:, 0, 0] + products[:, 1, 1]
    imag_part = products[:, 0, 1] - products[:, 1, 0]
    return jnp.stack([real_part, imag_part], axis=1)


def body(snapshots, closing, weights, bin_index):
    stride_rows = NFFT // 2
    tail_rows = closing.shape[0]
    blocks_here = snapshots.shape[0] // stride_rows
    points = snapshots.shape[1]
    width_tm = lax.axis_size("tm")
    width_space = lax.axis_size("space")
    blocks_all = blocks_here * width_tm
    own_rows = blocks_all // width_space
    basis_table = spectral_table(bin_index, NFFT)
    incoming = passed_along(snapshots[:tail_rows], "tm", -1)
    last_device = lax.axis_index("tm") == width_tm - 1
    series = jnp.concatenate([snapshots, jnp.where(last_device, closing, incoming)], axis=0)
    leading = series[: blocks_here * stride_rows].reshape(blocks_here, stride_rows, points)
    trailing = series[stride_rows:].reshape(blocks_here, stride_rows, points)
    pieces = jnp.concatenate([leading, trailing], axis=1)
    spectrum = jnp.einsum("nc,bnp->cbp", basis_table, pieces, precision=lax.Precision.HIGHEST)
    spectrum = spectrum.reshape(NBINS, 2, blocks_here, points)
    gathered = lax.all_to_all(spectrum, "tm", split_axis=0, concat_axis=2, tiled=True)
    weighted = gathered * weights
    summed = lax.psum_scatter(
        cross_spectra(gathered, weighted).transpose(2, 0, 1, 3),
        "space",
        scatter_dimension=0,
        tiled=True,
    )
    row_ids = lax.axis_index("space") * own_rows + jnp.arange(own_rows, dtype=jnp.int32)
    diagonal = (row_ids[:, None] == jnp.arange(blocks_all, dtype=jnp.int32)[None, :]).astype(
        jnp.float32
    )
    local_trace = jnp.einsum(
        "rkj,rj->k", summed[:, :, 0, :], diagonal, precision=lax.Precision.HIGHEST
    )
    energy = lax.psum(local_trace, "space")
    spectra = summed * (blocks_all / energy)[None, :, None, None]
    return spectra.transpose(1, 2, 0, 3)


def tile_start(device, tiles, width_tm, space):
    return (device * tiles + (space % 2) * (width_tm // 2)) // width_tm


def halves(value):
    high = value.astype(jnp.bfloat16)
    return high, (value - high.astype(jnp.float32)).astype(jnp.bfloat16)


def matmul(a, b):
    return lax.dot_general(a, b, (((1,), (0,)), ((), ())), preferred_element_type=jnp.float32)


def matmul_nt(a, b):
    return lax.dot_general(a, b, (((1,), (1,)), ((), ())), preferred_element_type=jnp.float32)


def picked(selector, values):
    high, low = halves(values)
    return matmul(selector, high) + matmul(selector, low)


def picked_right(values, selector):
    high, low = halves(values)
    return matmul(high, selector) + matmul(low, selector)


def table_rows(bins, length):
    shape = (bins.shape[0], length)
    sample = lax.broadcasted_iota(jnp.int32, shape, 1)
    odd = (lax.broadcasted_iota(jnp.int32, shape, 0) & 1) == 1
    window = 0.5 - 0.5 * jnp.cos(2.0 * jnp.pi * sample.astype(jnp.float32) / length)
    turns = (sample * bins) & (length - 1)
    angle = 2.0 * jnp.pi * turns.astype(jnp.float32) / length
    return window * jnp.where(odd, -jnp.sin(angle), jnp.cos(angle))


def selections(blocks, group, width_space):
    own = blocks // width_space
    size = blocks * group
    line = lax.broadcasted_iota(jnp.int32, (4 * blocks, size), 0)
    lane = lax.broadcasted_iota(jnp.int32, (4 * blocks, size), 1)
    second = line >= 2 * blocks
    row = line & (2 * blocks - 1)
    imag = (row // own) & 1
    match = row // (2 * own) * own + (row & (own - 1)) == lane // group
    wanted = jnp.where(second, 1 - imag, imag)
    sign = jnp.where((imag == 1) & ~second, -1.0, 1.0)
    left = jnp.where(match & ((lane & 1) == wanted), sign, 0.0)
    line = lax.broadcasted_iota(jnp.int32, (size, blocks * group // 2), 0)
    lane = lax.broadcasted_iota(jnp.int32, (size, blocks * group // 2), 1)
    place = line // group * (group // 2) + (line & (group - 1)) // 2 == lane
    even = jnp.where(place & ((line & 1) == 0), 1.0, 0.0)
    odd = jnp.where(place & ((line & 1) == 1), 1.0, 0.0)
    return [m.astype(jnp.bfloat16) for m in (left, even, odd)]


def over_blocks(row, bins):
    shift = row.shape[1] // 2
    while shift >= bins:
        row = row + pltpu.roll(row, shift, 1)
        shift //= 2
    return row


def kernel(
    n,
    n_space,
    snap_ref,
    closing_ref,
    weights_ref,
    bins_ref,
    out_ref,
    series,
    table_ref,
    left_ref,
    even_ref,
    odd_ref,
    a_high,
    a_low,
    b_high,
    b_low,
    gram,
    part,
    rows_in,
    weights,
    bins,
    local_sem,
    send_sem,
    recv_sem,
    part_send,
    part_recv,
    round_sem,
):
    me = lax.axis_index("tm")
    here = lax.axis_index("space")
    rows, points = snap_ref.shape
    tail_rows = closing_ref.shape[0]
    tiles = points // LANES
    steps = series.shape[0]
    pairs = steps - 1
    hop = NFFT // 2
    blocks_all = n * rows // hop
    channels = 2 * bins_ref.shape[0]
    group = channels // n
    own_rows = blocks_all // n_space

    deep = n // 2
    z, x = me // 2, lax.rem(me, 2)
    near = me // deep * deep
    far = deep - near

    def peer_of(k):
        return lax.rem(me + k, n)

    def begin(device):
        return tile_start(device, tiles, n, here)

    my_start = begin(me)
    my_last = begin(me + 1) - my_start == 2 * steps

    def rows_of(device):
        return pl.ds(pl.multiple_of(device * rows, rows), rows)

    def columns(start, count):
        return pl.ds(pl.multiple_of(start * LANES, LANES), count * LANES)

    def pair_copy(step, peer, sender):
        return pltpu.make_async_remote_copy(
            src_ref=snap_ref.at[:, columns(begin(peer) + 2 * step, 2)],
            dst_ref=series.at[step, rows_of(sender)],
            send_sem=send_sem.at[step, peer],
            recv_sem=recv_sem.at[step, sender],
            device_id={"tm": peer},
            device_id_type=MESH,
        )

    def half_copy(half, peer, sender):
        return pltpu.make_async_remote_copy(
            src_ref=snap_ref.at[:, columns(begin(peer) + 2 * pairs + half, 1)],
            dst_ref=series.at[pairs, rows_of(sender), pl.ds(half * LANES, LANES)],
            send_sem=send_sem.at[pairs + half, peer],
            recv_sem=recv_sem.at[pairs + half, sender],
            device_id={"tm": peer},
            device_id_type=MESH,
        )

    def has_last(device):
        return begin(device + 1) - begin(device) == 2 * steps

    def own_pair(step):
        source = columns(my_start + 2 * step, 2)
        return (
            pltpu.make_async_copy(
                snap_ref.at[:, source], series.at[step, rows_of(me)], local_sem.at[0, step]
            ),
            pltpu.make_async_copy(
                closing_ref.at[:, source],
                series.at[step, pl.ds(n * rows, tail_rows)],
                local_sem.at[1, step],
            ),
        )

    def own_half(half):
        source = columns(my_start + 2 * pairs + half, 1)
        lanes = pl.ds(half * LANES, LANES)
        return (
            pltpu.make_async_copy(
                snap_ref.at[:, source],
                series.at[pairs, rows_of(me), lanes],
                local_sem.at[0, pairs + half],
            ),
            pltpu.make_async_copy(
                closing_ref.at[:, source],
                series.at[pairs, pl.ds(n * rows, tail_rows), lanes],
                local_sem.at[1, pairs + half],
            ),
        )

    weights_copy = pltpu.make_async_copy(weights_ref, weights, local_sem.at[2, 0])
    bins_copy = pltpu.make_async_copy(bins_ref, bins, local_sem.at[2, 1])

    def greet(sem):
        pl.semaphore_signal(sem, inc=1, device_id={"tm": me + 1 - 2 * x}, device_id_type=MESH)

        @pl.when(z + 1 < deep)
        def _():
            pl.semaphore_signal(sem, inc=1, device_id={"tm": me + 2}, device_id_type=MESH)

        @pl.when(z > 0)
        def _():
            pl.semaphore_signal(sem, inc=1, device_id={"tm": me - 2}, device_id_type=MESH)

        for other in (here + 1 - 2 * lax.rem(here, 2), lax.rem(here + 2, n_space)):
            pl.semaphore_signal(sem, inc=1, device_id={"space": other}, device_id_type=MESH)
        pl.semaphore_wait(sem, 3 + (z + 1 < deep).astype(jnp.int32) + (z > 0).astype(jnp.int32))

    def hops(peer):
        return jnp.abs(peer // 2 - z) + jnp.abs(lax.rem(peer, 2) - x)

    for reach in range(1, deep + 1):
        greet(pltpu.get_barrier_semaphore() if reach == 1 else round_sem.at[reach - 2])
        for k in range(1, n):
            peer = peer_of(k)

            @pl.when(hops(peer) == reach)
            def _(peer=peer):
                pair_copy(0, peer, me).start()

    @pl.loop(1, pairs)
    def _(step):
        for k in range(1, n):
            pair_copy(step, peer_of(k), me).start()

    for k in range(1, n):
        half_copy(0, peer_of(k), me).start()
    for k in range(1, n):

        @pl.when(has_last(peer_of(k)))
        def _(k=k):
            half_copy(1, peer_of(k), me).start()

    @pl.loop(0, pairs)
    def _(step):
        for copy in own_pair(step):
            copy.start()

    for copy in own_half(0):
        copy.start()

    @pl.when(my_last)
    def _():
        for copy in own_half(1):
            copy.start()

    weights_copy.start()
    bins_copy.start()
    for reach in range(deep + 1, deep + 3):
        greet(round_sem.at[reach - 2])

    gram[...] = jnp.zeros(gram.shape, jnp.float32)
    left_ref[...], even_ref[...], odd_ref[...] = selections(blocks_all, group, n_space)
    bins_copy.wait()
    channel = lax.broadcasted_iota(jnp.int32, (channels, 1), 0)
    held = jnp.zeros((channels, 1), jnp.int32)
    for k in range(channels // 2):
        held = jnp.where(channel // 2 == k, bins[k], held)
    table_high, table_low = halves(table_rows(held, NFFT))
    table_ref[:channels] = table_high
    table_ref[channels:] = table_low
    weights_copy.wait()

    def transform(step, lanes, weight):
        def run(turn, carry):
            block = lax.rem(near * (rows // hop) + turn, blocks_all)
            window = pl.ds(pl.multiple_of(block * hop, hop), NFFT)
            high, low = halves(series[step, window, lanes])
            both = matmul(table_ref[...], high)
            coef = both[:channels] + both[channels:] + matmul(table_ref[:channels], low)
            first_high, first_low = halves(coef)
            second_high, second_low = halves(coef * weight)
            place = pl.ds(pl.multiple_of(block * group, group), group)
            for g in range(n):
                cut = slice(g * group, (g + 1) * group)
                a_high[g, place, lanes] = first_high[cut]
                a_low[g, place, lanes] = first_low[cut]
                b_high[g, place, lanes] = second_high[cut]
                b_low[g, place, lanes] = second_low[cut]
            return carry

        return run

    def products(lanes):
        def run(g, carry):
            gram[g] += (
                matmul_nt(b_high[g, :, lanes], a_high[g, :, lanes])
                + matmul_nt(b_high[g, :, lanes], a_low[g, :, lanes])
                + matmul_nt(b_low[g, :, lanes], a_high[g, :, lanes])
            )
            return carry

        lax.fori_loop(0, n, run, 0, unroll=2)

    ready = blocks_all // 2 - 1

    def near_peer(k):
        return near + lax.rem(me - near + k, deep)

    @pl.loop(0, pairs)
    def _(step):
        weight = weights[pl.ds(pl.multiple_of((my_start + 2 * step) * LANES, LANES), 2 * LANES)]
        run = transform(step, slice(0, 2 * LANES), weight.reshape(1, 2 * LANES))
        for copy in own_pair(step):
            copy.wait()
        for k in range(1, deep):
            pair_copy(step, me, near_peer(k)).wait_recv()
        lax.fori_loop(0, ready, run, 0, unroll=ready)
        for k in range(deep):
            pair_copy(step, me, far + k).wait_recv()
        lax.fori_loop(ready, blocks_all, run, 0, unroll=3)
        products(slice(0, 2 * LANES))

    def last(half):
        lanes = slice(half * LANES, (half + 1) * LANES)
        tile = my_start + 2 * pairs + half
        weight = weights[pl.ds(pl.multiple_of(tile * LANES, LANES), LANES)]
        run = transform(pairs, lanes, weight.reshape(1, LANES))
        for copy in own_half(half):
            copy.wait()
        for k in range(1, deep):
            half_copy(half, me, near_peer(k)).wait_recv()
        lax.fori_loop(0, ready, run, 0, unroll=ready)
        for k in range(deep):
            half_copy(half, me, far + k).wait_recv()
            stop = blocks_all if k == deep - 1 else ready + 2 + 2 * k
            first = ready + 2 * k
            lax.fori_loop(first, stop, run, 0, unroll=stop - first)
        products(lanes)

    last(0)

    @pl.when(my_last)
    def _():
        last(1)

    size = gram.shape[1]
    row = lax.broadcasted_iota(jnp.int32, (size, size), 0)
    col = lax.broadcasted_iota(jnp.int32, (size, size), 1)
    same_bin = ((row & (group - 1)) >> 1) == ((col & (group - 1)) >> 1)
    line = lax.broadcasted_iota(jnp.int32, part.shape[1:], 0)
    lane = lax.broadcasted_iota(jnp.int32, part.shape[1:], 1)
    imag_row = ((line // own_rows) & 1) == 1
    on_diagonal = line // (2 * own_rows) * own_rows + (line & (own_rows - 1)) == lane // (group // 2)

    def folded(g):
        kept = picked(left_ref[...], jnp.where(same_bin, gram[g], 0.0))
        middle = kept.shape[0] // 2
        sums = picked_right(kept[:middle], even_ref[...]) + picked_right(
            kept[middle:], odd_ref[...]
        )
        real = jnp.where(on_diagonal & ~imag_row, sums, 0.0)
        trace = over_blocks(jnp.sum(real, axis=0, keepdims=True), group // 2)
        part[g] = jnp.where(on_diagonal & imag_row, trace, sums)

    own_lines = 2 * own_rows

    def part_copy(peer, there, sender, sender_space):
        return pltpu.make_async_remote_copy(
            src_ref=part.at[peer, pl.ds(pl.multiple_of(there * own_lines, own_lines), own_lines)],
            dst_ref=rows_in.at[sender, sender_space],
            send_sem=part_send.at[peer, there],
            recv_sem=part_recv.at[sender, sender_space],
            device_id={"tm": peer, "space": there},
            device_id_type=MESH,
        )

    def others(k):
        return [lax.rem(here + j, n_space) for j in range(1 if k == 0 else 0, n_space)]

    order = [far + k for k in range(deep)] + [near_peer(k) for k in range(1, deep)]
    for peer in order:
        folded(peer)
        for there in others(1):
            part_copy(peer, there, me, here).start()
    folded(me)
    for there in others(0):
        part_copy(me, there, me, here).start()
    rows_in[me, here] = part[me, pl.ds(pl.multiple_of(here * own_lines, own_lines), own_lines)]
    for there in others(0):
        part_copy(me, here, me, there).wait_recv()
    for peer in order:
        for there in others(1):
            part_copy(me, here, peer, there).wait_recv()
    total = rows_in[0, 0]
    for p in range(n):
        for q in range(n_space):
            if p + q > 0:
                total = total + rows_in[p, q]
    line = lax.broadcasted_iota(jnp.int32, total.shape, 0)
    block = lax.broadcasted_iota(jnp.int32, total.shape, 1) // (group // 2)
    first = (line == own_rows) & (block == here * own_rows)
    held = jnp.sum(jnp.where(first, total, 0.0), axis=0, keepdims=True)
    energy = over_blocks(held, group // 2)
    zero = (line >= own_rows) & (block == here * own_rows + (line & (own_rows - 1)))
    out_ref[...] = jnp.where(zero, 0.0, total) * (blocks_all / energy)

    @pl.loop(0, pairs)
    def _(step):
        for k in range(1, n):
            pair_copy(step, peer_of(k), me).wait_send()

    for k in range(1, n):
        half_copy(0, peer_of(k), me).wait_send()

        @pl.when(has_last(peer_of(k)))
        def _(k=k):
            half_copy(1, peer_of(k), me).wait_send()

    for peer in order:
        for there in others(1):
            part_copy(peer, there, me, here).wait_send()
    for there in others(0):
        part_copy(me, there, me, here).wait_send()


def fused_body(snapshots, closing, weights, bin_index):
    n, n_space = lax.axis_size("tm"), lax.axis_size("space")
    rows, points = snapshots.shape
    tail_rows = closing.shape[0]
    tiles = points // LANES
    steps = -(-tiles // n) // 2
    blocks_all = n * rows // (NFFT // 2)
    channels = 2 * bin_index.shape[0]
    group = channels // n
    size = blocks_all * group
    own_rows = blocks_all // n_space
    shape = (2 * own_rows, size // 2)
    sums = pl.pallas_call(
        functools.partial(kernel, n, n_space),
        out_shape=jax.ShapeDtypeStruct(shape, jnp.float32),
        in_specs=[pl.BlockSpec(memory_space=pl.ANY)] * 4,
        out_specs=pl.BlockSpec(memory_space=pltpu.VMEM),
        scratch_shapes=[
            pltpu.VMEM((steps, n * rows + tail_rows, 2 * LANES), jnp.float32),
            pltpu.VMEM((2 * channels, NFFT), jnp.bfloat16),
            pltpu.VMEM((4 * blocks_all, size), jnp.bfloat16),
            pltpu.VMEM((size, size // 2), jnp.bfloat16),
            pltpu.VMEM((size, size // 2), jnp.bfloat16),
        ]
        + [pltpu.VMEM((n, size, 2 * LANES), jnp.bfloat16)] * 4
        + [
            pltpu.VMEM((n, size, size), jnp.float32),
            pltpu.VMEM((n, 2 * blocks_all, size // 2), jnp.float32),
            pltpu.VMEM((n, n_space) + shape, jnp.float32),
            pltpu.VMEM((points,), jnp.float32),
            pltpu.SMEM((channels // 2,), jnp.int32),
            pltpu.SemaphoreType.DMA((3, steps + 1)),
            pltpu.SemaphoreType.DMA((steps + 1, n)),
            pltpu.SemaphoreType.DMA((steps + 1, n)),
            pltpu.SemaphoreType.DMA((n, n_space)),
            pltpu.SemaphoreType.DMA((n, n_space)),
            pltpu.SemaphoreType.REGULAR((n // 2 + 1,)),
        ],
        compiler_params=pltpu.CompilerParams(collective_id=0, has_side_effects=True),
    )(snapshots, closing, weights, bin_index)
    by_pair = sums.reshape(2, own_rows, blocks_all, group // 2)
    return by_pair.transpose(3, 0, 1, 2)


def chosen_body(snapshots, closing, weights, bin_index):
    n, n_space = lax.axis_size("tm"), lax.axis_size("space")
    rows, points = snapshots.shape
    group = 2 * NBINS // n
    blocks_all = n * rows // (NFFT // 2)
    tiles = points // LANES
    slots = -(-tiles // n)
    fits = (
        2 * NBINS % n == 0
        and n % 2 == 0
        and n_space == 4
        and points % LANES == 0
        and slots % 2 == 0
        and slots > 2
        and tiles // n >= slots - 1
        and closing.shape[0] == NFFT // 2
        and rows == NFFT
        and group == 16
        and blocks_all == 16
    )
    return (fused_body if fits else body)(snapshots, closing, weights, bin_index)


def solution(mesh):
    return jax.shard_map(
        chosen_body,
        mesh=mesh,
        in_specs=(P("tm", "space"), P(None, "space"), P("space"), P()),
        out_specs=P("tm", None, "space", None),
        check_vma=False,
    )
```

time: 195 us -> 190 us (0.974)
  Pallas kernels: 191 us -> 188 us
    pallas_call x1, Pallas kernels: 191 us -> 188 us  [fused_body(): pl.pallas_call(functools.partial(kernel, n, n_space), out_shape=jax.Shape...]
where the time goes in v1:
time: 190 us
  Pallas kernels  188 us (99%)
    pallas_call x1, Pallas kernels, fused_body(): pl.pallas_call(functools.partial(kernel, n, n_space), out_shape=jax.Shape...  188 us

profile of v1, /device:TPU:0, one launch (start us, length us, event | category | flops | bytes accessed | tf_op | source)
XLA Modules:
  0.0 190.0 jit_solution(5682601017111768864)
XLA Ops:
  0.0 188.5 %shard_map.46 = f32[8,128]{1,0:T(8,128)} custom-call(f32[256,7680]{1,0:T(8,128)} %snap_ref.1, f32[128,7680]{1,0:T(8,128)} %closing_ref.1, f32[7680]{0:T(1024)} %weights_ref.1, s32[64]{0:T(128)} %bins_ref.1), custom_call_target="tpu_custom_call" | custom-call | tf_op jit(solution)/shard_map/pallas_call | solution.py:497
  188.5 0.8 reshape.3
  189.3 0.7 copy.6

commit v2 on v1

v2 whole, which is shorter than its diff:
```python
import functools

import jax
import jax.numpy as jnp
from jax import lax
from jax.experimental import pallas as pl
from jax.experimental.pallas import tpu as pltpu
from jax.sharding import PartitionSpec as P

NFFT = 256
NBINS = 64
LANES = 128
MESH = pl.DeviceIdType.MESH


def passed_along(array, axis, by):
    peers = lax.axis_size(axis)
    pairs = [(i, i + by) for i in range(peers) if 0 <= i + by < peers]
    return lax.ppermute(array, axis, pairs)


def spectral_table(bin_index, length):
    sample = jnp.arange(length, dtype=jnp.int32)
    window = 0.5 - 0.5 * jnp.cos(2.0 * jnp.pi * sample.astype(jnp.float32) / length)
    phase_turns = sample[:, None] * bin_index[None, :] % length
    phase_angle = 2.0 * jnp.pi * phase_turns.astype(jnp.float32) / length
    paired = jnp.stack(
        [window[:, None] * jnp.cos(phase_angle), -window[:, None] * jnp.sin(phase_angle)], axis=2
    )
    return paired.reshape(length, 2 * bin_index.shape[0])


def cross_spectra(first_set, second_set):
    products = jnp.einsum(
        "kaip,kbjp->kabij", first_set, second_set, precision=lax.Precision.HIGHEST
    )
    real_part = products[:, 0, 0] + products[:, 1, 1]
    imag_part = products[:, 0, 1] - products[:, 1, 0]
    return jnp.stack([real_part, imag_part], axis=1)


def body(snapshots, closing, weights, bin_index):
    stride_rows = NFFT // 2
    tail_rows = closing.shape[0]
    blocks_here = snapshots.shape[0] // stride_rows
    points = snapshots.shape[1]
    width_tm = lax.axis_size("tm")
    width_space = lax.axis_size("space")
    blocks_all = blocks_here * width_tm
    own_rows = blocks_all // width_space
    basis_table = spectral_table(bin_index, NFFT)
    incoming = passed_along(snapshots[:tail_rows], "tm", -1)
    last_device = lax.axis_index("tm") == width_tm - 1
    series = jnp.concatenate([snapshots, jnp.where(last_device, closing, incoming)], axis=0)
    leading = series[: blocks_here * stride_rows].reshape(blocks_here, stride_rows, points)
    trailing = series[stride_rows:].reshape(blocks_here, stride_rows, points)
    pieces = jnp.concatenate([leading, trailing], axis=1)
    spectrum = jnp.einsum("nc,bnp->cbp", basis_table, pieces, precision=lax.Precision.HIGHEST)
    spectrum = spectrum.reshape(NBINS, 2, blocks_here, points)
    gathered = lax.all_to_all(spectrum, "tm", split_axis=0, concat_axis=2, tiled=True)
    weighted = gathered * weights
    summed = lax.psum_scatter(
        cross_spectra(gathered, weighted).transpose(2, 0, 1, 3),
        "space",
        scatter_dimension=0,
        tiled=True,
    )
    row_ids = lax.axis_index("space") * own_rows + jnp.arange(own_rows, dtype=jnp.int32)
    diagonal = (row_ids[:, None] == jnp.arange(blocks_all, dtype=jnp.int32)[None, :]).astype(
        jnp.float32
    )
    local_trace = jnp.einsum(
        "rkj,rj->k", summed[:, :, 0, :], diagonal, precision=lax.Precision.HIGHEST
    )
    energy = lax.psum(local_trace, "space")
    spectra = summed * (blocks_all / energy)[None, :, None, None]
    return spectra.transpose(1, 2, 0, 3)


def halves(value):
    high = value.astype(jnp.bfloat16)
    return high, (value - high.astype(jnp.float32)).astype(jnp.bfloat16)


def matmul(a, b):
    return lax.dot_general(a, b, (((1,), (0,)), ((), ())), preferred_element_type=jnp.float32)


def matmul_nt(a, b):
    return lax.dot_general(a, b, (((1,), (1,)), ((), ())), preferred_element_type=jnp.float32)


def picked(selector, values):
    high, low = halves(values)
    return matmul(selector, high) + matmul(selector, low)


def picked_right(values, selector):
    high, low = halves(values)
    return matmul(high, selector) + matmul(low, selector)


def table_rows(bins, length):
    shape = (bins.shape[0], length)
    sample = lax.broadcasted_iota(jnp.int32, shape, 1)
    odd = (lax.broadcasted_iota(jnp.int32, shape, 0) & 1) == 1
    window = 0.5 - 0.5 * jnp.cos(2.0 * jnp.pi * sample.astype(jnp.float32) / length)
    turns = (sample * bins) & (length - 1)
    angle = 2.0 * jnp.pi * turns.astype(jnp.float32) / length
    return window * jnp.where(odd, -jnp.sin(angle), jnp.cos(angle))


def selections(blocks, group, width_space):
    own = blocks // width_space
    size = blocks * group
    line = lax.broadcasted_iota(jnp.int32, (4 * blocks, size), 0)
    lane = lax.broadcasted_iota(jnp.int32, (4 * blocks, size), 1)
    second = line >= 2 * blocks
    row = line & (2 * blocks - 1)
    imag = (row // own) & 1
    match = row // (2 * own) * own + (row & (own - 1)) == lane // group
    wanted = jnp.where(second, 1 - imag, imag)
    sign = jnp.where((imag == 1) & ~second, -1.0, 1.0)
    left = jnp.where(match & ((lane & 1) == wanted), sign, 0.0)
    line = lax.broadcasted_iota(jnp.int32, (size, blocks * group // 2), 0)
    lane = lax.broadcasted_iota(jnp.int32, (size, blocks * group // 2), 1)
    place = line // group * (group // 2) + (line & (group - 1)) // 2 == lane
    even = jnp.where(place & ((line & 1) == 0), 1.0, 0.0)
    odd = jnp.where(place & ((line & 1) == 1), 1.0, 0.0)
    return [m.astype(jnp.bfloat16) for m in (left, even, odd)]


def over_blocks(row, bins):
    shift = row.shape[1] // 2
    while shift >= bins:
        row = row + pltpu.roll(row, shift, 1)
        shift //= 2
    return row


def kernel(
    n,
    n_space,
    snap_ref,
    closing_ref,
    weights_ref,
    bins_ref,
    out_ref,
    series,
    late_series,
    table_ref,
    left_ref,
    even_ref,
    odd_ref,
    a_high,
    a_low,
    b_high,
    b_low,
    late_a_high,
    late_a_low,
    late_b_high,
    late_b_low,
    gram,
    coef_out,
    coef_in,
    edge_out,
    edge_in,
    part,
    space_in,
    rows_out,
    rows_in,
    late_part,
    late_in,
    weights,
    bins,
    local_sem,
    send_sem,
    recv_sem,
    halo_sem,
    space_send,
    space_recv,
    rows_send,
    rows_recv,
    late_send,
    late_recv,
    round_sem,
):
    me = lax.axis_index("tm")
    here = lax.axis_index("space")
    rows, points = snap_ref.shape
    tail_rows = closing_ref.shape[0]
    tiles = points // LANES
    each = tiles // n
    pairs = each // 2
    late_tiles = tiles - each * n
    hop = NFFT // 2
    blocks_here = rows // hop
    blocks_all = n * blocks_here
    channels = 2 * bins_ref.shape[0]
    group = channels // n
    own_rows = blocks_all // n_space
    own_lines = 2 * own_rows
    held_rows = blocks_here * group

    deep = n // 2
    z, x = me // 2, lax.rem(me, 2)
    near = me // deep * deep
    far = deep - near
    near_peers = [near + lax.rem(me - near + k, deep) for k in range(1, deep)]
    far_peers = [far + lax.rem(me - near + k, deep) for k in range(deep)]
    peers = far_peers + near_peers
    space_peers = [lax.rem(here + k, n_space) for k in range(1, n_space)]

    def rows_of(device):
        return pl.ds(pl.multiple_of(device * rows, rows), rows)

    def columns(start, count):
        return pl.ds(pl.multiple_of(start * LANES, LANES), count * LANES)

    late_columns = pl.ds(each * n * LANES, late_tiles * LANES)

    def to_tm(src, dst, kind, peer, sender):
        return pltpu.make_async_remote_copy(
            src_ref=src,
            dst_ref=dst,
            send_sem=send_sem.at[kind, peer],
            recv_sem=recv_sem.at[kind, sender],
            device_id={"tm": peer},
            device_id_type=MESH,
        )

    def pair_copy(step, peer, sender):
        source = columns(peer * each + 2 * step, 2)
        return to_tm(
            snap_ref.at[:, source], series.at[step, rows_of(sender)], step, peer, sender
        )

    def single_copy(peer, sender):
        source = columns(peer * each + 2 * pairs, 1)
        target = series.at[pairs, rows_of(sender), pl.ds(0, LANES)]
        return to_tm(snap_ref.at[:, source], target, pairs, peer, sender)

    def coef_copy(peer, sender):
        target = coef_in.at[pl.ds(pl.multiple_of(sender * held_rows, held_rows), held_rows)]
        return to_tm(coef_out.at[peer], target, pairs + 1, peer, sender)

    def edge_copy(peer):
        return to_tm(edge_out.at[peer], edge_in, pairs + 2, peer, deep)

    halo_copy = pltpu.make_async_remote_copy(
        src_ref=snap_ref.at[pl.ds(0, tail_rows), late_columns],
        dst_ref=late_series.at[pl.ds(rows, tail_rows)],
        send_sem=halo_sem.at[0],
        recv_sem=halo_sem.at[1],
        device_id={"tm": lax.rem(me + n - 1, n)},
        device_id_type=MESH,
    )
    gives_halo = (me != 0) & (me != deep)
    takes_halo = (me != n - 1) & (me != deep - 1)

    def own_copies(step):
        single = isinstance(step, int) and step == pairs
        source = columns(me * each + 2 * step, 1 if single else 2)
        lanes = pl.ds(0, LANES if single else 2 * LANES)
        return (
            pltpu.make_async_copy(
                snap_ref.at[:, source], series.at[step, rows_of(me), lanes], local_sem.at[0, step]
            ),
            pltpu.make_async_copy(
                closing_ref.at[:, source],
                series.at[step, pl.ds(n * rows, tail_rows), lanes],
                local_sem.at[1, step],
            ),
        )

    late_own = pltpu.make_async_copy(
        snap_ref.at[:, late_columns], late_series.at[pl.ds(0, rows)], local_sem.at[2, 0]
    )
    late_closing = pltpu.make_async_copy(
        closing_ref.at[:, late_columns],
        late_series.at[pl.ds(rows, tail_rows)],
        local_sem.at[2, 1],
    )
    weights_copy = pltpu.make_async_copy(weights_ref, weights, local_sem.at[2, 2])
    bins_copy = pltpu.make_async_copy(bins_ref, bins, local_sem.at[2, 3])

    def greet(sem):
        pl.semaphore_signal(sem, inc=1, device_id={"tm": me + 1 - 2 * x}, device_id_type=MESH)

        @pl.when(z + 1 < deep)
        def _():
            pl.semaphore_signal(sem, inc=1, device_id={"tm": me + 2}, device_id_type=MESH)

        @pl.when(z > 0)
        def _():
            pl.semaphore_signal(sem, inc=1, device_id={"tm": me - 2}, device_id_type=MESH)

        for other in (here + 1 - 2 * lax.rem(here, 2), lax.rem(here + 2, n_space)):
            pl.semaphore_signal(sem, inc=1, device_id={"space": other}, device_id_type=MESH)
        pl.semaphore_wait(sem, 3 + (z + 1 < deep).astype(jnp.int32) + (z > 0).astype(jnp.int32))

    def hops(peer):
        return jnp.abs(peer // 2 - z) + jnp.abs(lax.rem(peer, 2) - x)

    for reach in range(1, deep + 1):
        greet(pltpu.get_barrier_semaphore() if reach == 1 else round_sem.at[reach - 2])
        for peer in peers:

            @pl.when(hops(peer) == reach)
            def _(peer=peer):
                pair_copy(0, peer, me).start()

        if reach == 2:

            @pl.when(gives_halo)
            def _():
                halo_copy.start()

    for step in range(1, pairs):
        for peer in near_peers + far_peers:
            pair_copy(step, peer, me).start()
    for peer in near_peers:
        single_copy(peer, me).start()

    bins_copy.start()
    late_own.start()

    @pl.when(me == n - 1)
    def _():
        late_closing.start()

    weights_copy.start()

    for step in range(pairs + 1):
        for copy in own_copies(step):
            copy.start()

    @pl.when(me == deep - 1)
    def _():
        late_series[rows:] = jnp.zeros((tail_rows, late_series.shape[1]), jnp.float32)

    gram[...] = jnp.zeros(gram.shape, jnp.float32)
    left_ref[...], even_ref[...], odd_ref[...] = selections(blocks_all, group, n_space)
    bins_copy.wait()
    channel = lax.broadcasted_iota(jnp.int32, (channels, 1), 0)
    held = jnp.zeros((channels, 1), jnp.int32)
    for k in range(channels // 2):
        held = jnp.where(channel // 2 == k, bins[k], held)
    table_high, table_low = halves(table_rows(held, NFFT))
    table_ref[:channels] = table_high
    table_ref[channels:] = table_low
    weights_copy.wait()

    def transformed(piece):
        high, low = halves(piece)
        both = matmul(table_ref[...], high)
        return both[:channels] + both[channels:] + matmul(table_ref[:channels], low)

    late_own.wait()

    @pl.when(takes_halo)
    def _():
        halo_copy.wait_recv()

    @pl.when(me == n - 1)
    def _():
        late_closing.wait()

    for block in range(blocks_here):
        coef = transformed(late_series[block * hop : block * hop + NFFT])
        for g in range(n):
            coef_out[g, block * group : (block + 1) * group] = coef[g * group : (g + 1) * group]
    coef_in[pl.ds(pl.multiple_of(me * held_rows, held_rows), held_rows)] = coef_out[me]

    @pl.when(me == deep)
    def _():
        begun = late_series[:hop]
        coef = transformed(jnp.concatenate([jnp.zeros_like(begun), begun], axis=0))
        for g in range(n):
            edge_out[g] = coef[g * group : (g + 1) * group]
        edge_in[...] = edge_out[me]

    def transform(step, lanes, weight):
        def run(turn, carry):
            block = lax.rem(near * blocks_here + turn, blocks_all)
            window = pl.ds(pl.multiple_of(block * hop, hop), NFFT)
            coef = transformed(series[step, window, lanes])
            first_high, first_low = halves(coef)
            second_high, second_low = halves(coef * weight)
            place = pl.ds(pl.multiple_of(block * group, group), group)
            for g in range(n):
                cut = slice(g * group, (g + 1) * group)
                a_high[g, place, lanes] = first_high[cut]
                a_low[g, place, lanes] = first_low[cut]
                b_high[g, place, lanes] = second_high[cut]
                b_low[g, place, lanes] = second_low[cut]
            return carry

        return run

    def products(lanes):
        def run(g, carry):
            gram[g] += (
                matmul_nt(b_high[g, :, lanes], a_high[g, :, lanes])
                + matmul_nt(b_high[g, :, lanes], a_low[g, :, lanes])
                + matmul_nt(b_low[g, :, lanes], a_high[g, :, lanes])
            )
            return carry

        lax.fori_loop(0, n, run, 0, unroll=2)

    ready = blocks_all // 2 - 1

    @pl.loop(0, pairs)
    def _(step):
        @pl.when(step == 1)
        def _():
            for peer in near_peers:
                coef_copy(peer, me).start()

            @pl.when(me == deep)
            def _():
                for peer in near_peers:
                    edge_copy(peer).start()

            for peer in far_peers:
                single_copy(peer, me).start()
            for peer in far_peers:
                coef_copy(peer, me).start()

            @pl.when(me == deep)
            def _():
                for peer in far_peers:
                    edge_copy(peer).start()

        start = pl.multiple_of((me * each + 2 * step) * LANES, LANES)
        weight = weights[pl.ds(start, 2 * LANES)].reshape(1, 2 * LANES)
        run = transform(step, slice(0, 2 * LANES), weight)
        for copy in own_copies(step):
            copy.wait()
        for peer in near_peers:
            pair_copy(step, me, peer).wait_recv()
        lax.fori_loop(0, ready, run, 0, unroll=ready)
        for k in range(deep):
            pair_copy(step, me, far + k).wait_recv()
        lax.fori_loop(ready, blocks_all, run, 0, unroll=3)
        products(slice(0, 2 * LANES))

    start = pl.multiple_of((me * each + 2 * pairs) * LANES, LANES)
    run = transform(pairs, slice(0, LANES), weights[pl.ds(start, LANES)].reshape(1, LANES))
    for copy in own_copies(pairs):
        copy.wait()
    for peer in near_peers:
        single_copy(me, peer).wait_recv()
    lax.fori_loop(0, ready, run, 0, unroll=ready)
    for k in range(deep):
        single_copy(me, far + k).wait_recv()
        stop = blocks_all if k == deep - 1 else ready + 2 + 2 * k
        first = ready + 2 * k
        lax.fori_loop(first, stop, run, 0, unroll=stop - first)
    products(slice(0, LANES))

    size = gram.shape[1]
    row = lax.broadcasted_iota(jnp.int32, (size, size), 0)
    col = lax.broadcasted_iota(jnp.int32, (size, size), 1)
    same_bin = ((row & (group - 1)) >> 1) == ((col & (group - 1)) >> 1)
    line = lax.broadcasted_iota(jnp.int32, late_part.shape, 0)
    lane = lax.broadcasted_iota(jnp.int32, late_part.shape, 1)
    imag_row = ((line // own_rows) & 1) == 1
    on_diagonal = line // own_lines * own_rows + (line & (own_rows - 1)) == lane // (group // 2)

    def folded(values):
        kept = picked(left_ref[...], jnp.where(same_bin, values, 0.0))
        middle = kept.shape[0] // 2
        sums = picked_right(kept[:middle], even_ref[...]) + picked_right(
            kept[middle:], odd_ref[...]
        )
        real = jnp.where(on_diagonal & ~imag_row, sums, 0.0)
        trace = over_blocks(jnp.sum(real, axis=0, keepdims=True), group // 2)
        return jnp.where(on_diagonal & imag_row, trace, sums)

    def fold(g, carry):
        sums = folded(gram[g])
        for s in range(n_space):
            part[s, g] = sums[s * own_lines : (s + 1) * own_lines]
        return carry

    lax.fori_loop(0, n, fold, 0, unroll=2)

    def space_copy(peer, sender):
        return pltpu.make_async_remote_copy(
            src_ref=part.at[peer],
            dst_ref=space_in.at[sender],
            send_sem=space_send.at[peer],
            recv_sem=space_recv.at[sender],
            device_id={"space": peer},
            device_id_type=MESH,
        )

    def rows_copy(peer, sender):
        return pltpu.make_async_remote_copy(
            src_ref=rows_out.at[peer],
            dst_ref=rows_in.at[sender],
            send_sem=rows_send.at[peer],
            recv_sem=rows_recv.at[sender],
            device_id={"tm": peer},
            device_id_type=MESH,
        )

    def late_copy(peer, sender):
        source = pl.ds(pl.multiple_of(peer * own_lines, own_lines), own_lines)
        return pltpu.make_async_remote_copy(
            src_ref=late_part.at[source],
            dst_ref=late_in.at[sender],
            send_sem=late_send.at[peer],
            recv_sem=late_recv.at[sender],
            device_id={"space": peer},
            device_id_type=MESH,
        )

    for peer in space_peers:
        space_copy(peer, here).start()
    space_in[here] = part[here]
    for peer in space_peers:
        space_copy(here, peer).wait_recv()
    total = space_in[0]
    for s in range(1, n_space):
        total = total + space_in[s]
    rows_out[...] = total
    rows_in[me] = rows_out[me]
    for peer in peers:
        rows_copy(peer, me).start()

    late_weight = weights[pl.ds(each * n * LANES, late_tiles * LANES)]
    late_weight = late_weight.reshape(1, late_tiles * LANES)

    def take(sender, straddles=False):
        @pl.when(sender != me)
        def _():
            coef_copy(me, sender).wait_recv()

        place = pl.ds(pl.multiple_of(sender * held_rows, held_rows), held_rows)
        coef = coef_in[place]
        if straddles:

            @pl.when(me != deep)
            def _():
                edge_copy(me).wait_recv()

            coef = jnp.concatenate(
                [coef[: held_rows - group], coef[held_rows - group :] + edge_in[...]], axis=0
            )
        late_a_high[place], late_a_low[place] = halves(coef)
        late_b_high[place], late_b_low[place] = halves(coef * late_weight)

    for k in range(deep - 1):
        take(near + k)
    for k in range(deep - 1):
        take(far + k)
    take(jnp.int32(n - 1))
    take(jnp.int32(deep - 1), straddles=True)
    late_part[...] = folded(
        matmul_nt(late_b_high[...], late_a_high[...])
        + matmul_nt(late_b_high[...], late_a_low[...])
        + matmul_nt(late_b_low[...], late_a_high[...])
    )
    for peer in space_peers:
        late_copy(peer, here).start()
    late_in[here] = late_part[pl.ds(pl.multiple_of(here * own_lines, own_lines), own_lines)]
    for peer in peers:
        rows_copy(me, peer).wait_recv()
    total = rows_in[0]
    for p in range(1, n):
        total = total + rows_in[p]
    for peer in space_peers:
        late_copy(here, peer).wait_recv()
    for s in range(n_space):
        total = total + late_in[s]
    line = lax.broadcasted_iota(jnp.int32, total.shape, 0)
    block = lax.broadcasted_iota(jnp.int32, total.shape, 1) // (group // 2)
    first = (line == own_rows) & (block == here * own_rows)
    held = jnp.sum(jnp.where(first, total, 0.0), axis=0, keepdims=True)
    energy = over_blocks(held, group // 2)
    zero = (line >= own_rows) & (block == here * own_rows + (line & (own_rows - 1)))
    out_ref[...] = jnp.where(zero, 0.0, total) * (blocks_all / energy)

    for peer in peers:
        for step in range(pairs):
            pair_copy(step, peer, me).wait_send()
        single_copy(peer, me).wait_send()
        coef_copy(peer, me).wait_send()
        rows_copy(peer, me).wait_send()

    @pl.when(gives_halo)
    def _():
        halo_copy.wait_send()

    @pl.when(me == deep)
    def _():
        for peer in peers:
            edge_copy(peer).wait_send()

    for peer in space_peers:
        space_copy(peer, here).wait_send()
        late_copy(peer, here).wait_send()


def fused_body(snapshots, closing, weights, bin_index):
    n, n_space = lax.axis_size("tm"), lax.axis_size("space")
    rows, points = snapshots.shape
    tail_rows = closing.shape[0]
    tiles = points // LANES
    each = tiles // n
    pairs = each // 2
    late = (tiles - each * n) * LANES
    blocks_all = n * rows // (NFFT // 2)
    channels = 2 * bin_index.shape[0]
    group = channels // n
    size = blocks_all * group
    own_lines = 2 * blocks_all // n_space
    shape = (own_lines, size // 2)
    sums = pl.pallas_call(
        functools.partial(kernel, n, n_space),
        out_shape=jax.ShapeDtypeStruct(shape, jnp.float32),
        in_specs=[pl.BlockSpec(memory_space=pl.ANY)] * 4,
        out_specs=pl.BlockSpec(memory_space=pltpu.VMEM),
        scratch_shapes=[
            pltpu.VMEM((pairs + 1, n * rows + tail_rows, 2 * LANES), jnp.float32),
            pltpu.VMEM((rows + tail_rows, late), jnp.float32),
            pltpu.VMEM((2 * channels, NFFT), jnp.bfloat16),
            pltpu.VMEM((4 * blocks_all, size), jnp.bfloat16),
            pltpu.VMEM((size, size // 2), jnp.bfloat16),
            pltpu.VMEM((size, size // 2), jnp.bfloat16),
        ]
        + [pltpu.VMEM((n, size, 2 * LANES), jnp.bfloat16)] * 4
        + [pltpu.VMEM((size, late), jnp.bfloat16)] * 4
        + [
            pltpu.VMEM((n, size, size), jnp.float32),
            pltpu.VMEM((n, size // n, late), jnp.float32),
            pltpu.VMEM((size, late), jnp.float32),
            pltpu.VMEM((n, group, late), jnp.float32),
            pltpu.VMEM((group, late), jnp.float32),
            pltpu.VMEM((n_space, n) + shape, jnp.float32),
            pltpu.VMEM((n_space, n) + shape, jnp.float32),
            pltpu.VMEM((n,) + shape, jnp.float32),
            pltpu.VMEM((n,) + shape, jnp.float32),
            pltpu.VMEM((n_space * own_lines, size // 2), jnp.float32),
            pltpu.VMEM((n_space,) + shape, jnp.float32),
            pltpu.VMEM((points,), jnp.float32),
            pltpu.SMEM((channels // 2,), jnp.int32),
            pltpu.SemaphoreType.DMA((3, max(4, pairs + 1))),
            pltpu.SemaphoreType.DMA((pairs + 3, n)),
            pltpu.SemaphoreType.DMA((pairs + 3, n)),
            pltpu.SemaphoreType.DMA((2,)),
            pltpu.SemaphoreType.DMA((n_space,)),
            pltpu.SemaphoreType.DMA((n_space,)),
            pltpu.SemaphoreType.DMA((n,)),
            pltpu.SemaphoreType.DMA((n,)),
            pltpu.SemaphoreType.DMA((n_space,)),
            pltpu.SemaphoreType.DMA((n_space,)),
            pltpu.SemaphoreType.REGULAR((n // 2 - 1,)),
        ],
        compiler_params=pltpu.CompilerParams(collective_id=0, has_side_effects=True),
    )(snapshots, closing, weights, bin_index)
    by_pair = sums.reshape(2, own_lines // 2, blocks_all, group // 2)
    return by_pair.transpose(3, 0, 1, 2)


def chosen_body(snapshots, closing, weights, bin_index):
    n, n_space = lax.axis_size("tm"), lax.axis_size("space")
    rows, points = snapshots.shape
    group = 2 * NBINS // n
    blocks_all = n * rows // (NFFT // 2)
    tiles = points // LANES
    fits = (
        2 * NBINS % n == 0
        and n % 2 == 0
        and n_space == 4
        and points % LANES == 0
        and tiles // n % 2 == 1
        and tiles // n > 2
        and tiles % n > 0
        and closing.shape[0] == NFFT // 2
        and rows == NFFT
        and group == 16
        and blocks_all == 16
    )
    return (fused_body if fits else body)(snapshots, closing, weights, bin_index)


def solution(mesh):
    return jax.shard_map(
        chosen_body,
        mesh=mesh,
        in_specs=(P("tm", "space"), P(None, "space"), P("space"), P()),
        out_specs=P("tm", None, "space", None),
        check_vma=False,
    )
```

time: 190 us -> 191 us (level)
  Pallas kernels: 188 us -> 190 us
where the time goes in v2:
time: 191 us
  Pallas kernels  190 us (99%)
    pallas_call x1, Pallas kernels, fused_body(): pl.pallas_call(functools.partial(kernel, n, n_space), out_shape=jax.Shape...  190 us

profile of v2, /device:TPU:0, one launch (start us, length us, event | category | flops | bytes accessed | tf_op | source)
XLA Modules:
  0.0 191.2 jit_solution(18034434575238782122)
XLA Ops:
  0.0 189.7 %shard_map.46 = f32[8,128]{1,0:T(8,128)} custom-call(f32[256,7680]{1,0:T(8,128)} %snap_ref.1, f32[128,7680]{1,0:T(8,128)} %closing_ref.1, f32[7680]{0:T(1024)} %weights_ref.1, s32[64]{0:T(128)} %bins_ref.1), custom_call_target="tpu_custom_call" | custom-call | tf_op jit(solution)/shard_map/pallas_call | solution.py:622
  189.7 0.8 reshape.3
  190.5 0.7 copy.6

commit v3 on v1

--- a/solution.py
+++ b/solution.py
@@ -128,16 +128,20 @@
     left = jnp.where(match & ((lane & 1) == wanted), sign, 0.0)
     line = lax.broadcasted_iota(jnp.int32, (size, blocks * group // 2), 0)
     lane = lax.broadcasted_iota(jnp.int32, (size, blocks * group // 2), 1)
-    place = line // group * (group // 2) + (line & (group - 1)) // 2 == lane
+    place = (line // group == lane & (blocks - 1)) & ((line & (group - 1)) // 2 == lane // blocks)
     even = jnp.where(place & ((line & 1) == 0), 1.0, 0.0)
     odd = jnp.where(place & ((line & 1) == 1), 1.0, 0.0)
     return [m.astype(jnp.bfloat16) for m in (left, even, odd)]
 
 
-def over_blocks(row, bins):
-    shift = row.shape[1] // 2
-    while shift >= bins:
-        row = row + pltpu.roll(row, shift, 1)
+def over_blocks(row, blocks):
+    lane = lax.broadcasted_iota(jnp.int32, row.shape, 1)
+    width = row.shape[1]
+    shift = blocks // 2
+    while shift > 0:
+        up = pltpu.roll(row, shift, 1)
+        down = pltpu.roll(row, width - shift, 1)
+        row = row + jnp.where((lane & shift) == 0, down, up)
         shift //= 2
     return row
 
@@ -160,6 +164,7 @@
     b_high,
     b_low,
     gram,
+    final,
     part,
     rows_in,
     weights,
@@ -329,7 +334,7 @@
     table_ref[channels:] = table_low
     weights_copy.wait()
 
-    def transform(step, lanes, weight):
+    def transform(step, lanes, weight, half=False):
         def run(turn, carry):
             block = lax.rem(near * (rows // hop) + turn, blocks_all)
             window = pl.ds(pl.multiple_of(block * hop, hop), NFFT)
@@ -341,24 +346,33 @@
             place = pl.ds(pl.multiple_of(block * group, group), group)
             for g in range(n):
                 cut = slice(g * group, (g + 1) * group)
-                a_high[g, place, lanes] = first_high[cut]
-                a_low[g, place, lanes] = first_low[cut]
-                b_high[g, place, lanes] = second_high[cut]
-                b_low[g, place, lanes] = second_low[cut]
+                if half:
+                    a_high[g, place, :LANES] = first_high[cut]
+                    a_high[g, place, LANES:] = first_low[cut]
+                    b_high[g, place, :LANES] = second_high[cut]
+                    b_low[g, place, :LANES] = second_low[cut]
+                else:
+                    a_high[g, place, :] = first_high[cut]
+                    a_low[g, place, :] = first_low[cut]
+                    b_high[g, place, :] = second_high[cut]
+                    b_low[g, place, :] = second_low[cut]
             return carry
 
         return run
 
-    def products(lanes):
-        def run(g, carry):
-            gram[g] += (
-                matmul_nt(b_high[g, :, lanes], a_high[g, :, lanes])
-                + matmul_nt(b_high[g, :, lanes], a_low[g, :, lanes])
-                + matmul_nt(b_low[g, :, lanes], a_high[g, :, lanes])
-            )
-            return carry
-
-        lax.fori_loop(0, n, run, 0, unroll=2)
+    def products(g, carry):
+        gram[g] += (
+            matmul_nt(b_high[g], a_high[g])
+            + matmul_nt(b_high[g], a_low[g])
+            + matmul_nt(b_low[g], a_high[g])
+        )
+        return carry
+
+    def half_product(g):
+        first, second = a_high[g], b_high[g, :, :LANES]
+        return matmul_nt(jnp.concatenate([second, second], axis=1), first) + matmul_nt(
+            b_low[g, :, :LANES], first[:, :LANES]
+        )
 
     ready = blocks_all // 2 - 1
 
@@ -377,13 +391,13 @@
         for k in range(deep):
             pair_copy(step, me, far + k).wait_recv()
         lax.fori_loop(ready, blocks_all, run, 0, unroll=3)
-        products(slice(0, 2 * LANES))
+        lax.fori_loop(0, n, products, 0, unroll=2)
 
     def last(half):
         lanes = slice(half * LANES, (half + 1) * LANES)
         tile = my_start + 2 * pairs + half
         weight = weights[pl.ds(pl.multiple_of(tile * LANES, LANES), LANES)]
-        run = transform(pairs, lanes, weight.reshape(1, LANES))
+        run = transform(pairs, lanes, weight.reshape(1, LANES), half=True)
         for copy in own_half(half):
             copy.wait()
         for k in range(1, deep):
@@ -394,13 +408,14 @@
             stop = blocks_all if k == deep - 1 else ready + 2 + 2 * k
             first = ready + 2 * k
             lax.fori_loop(first, stop, run, 0, unroll=stop - first)
-        products(lanes)
 
     last(0)
 
-    @pl.when(my_last)
-    def _():
-        last(1)
+    def half_products(g, carry):
+        gram[g] += half_product(g)
+        return carry
+
+    lax.fori_loop(0, n, half_products, 0, unroll=2)
 
     size = gram.shape[1]
     row = lax.broadcasted_iota(jnp.int32, (size, size), 0)
@@ -409,59 +424,85 @@
     line = lax.broadcasted_iota(jnp.int32, part.shape[1:], 0)
     lane = lax.broadcasted_iota(jnp.int32, part.shape[1:], 1)
     imag_row = ((line // own_rows) & 1) == 1
-    on_diagonal = line // (2 * own_rows) * own_rows + (line & (own_rows - 1)) == lane // (group // 2)
-
-    def folded(g):
-        kept = picked(left_ref[...], jnp.where(same_bin, gram[g], 0.0))
+    held_row = line // (2 * own_rows) * own_rows + (line & (own_rows - 1))
+    on_diagonal = held_row == lane & (blocks_all - 1)
+
+    def fold(k):
+        kept = picked(left_ref[...], jnp.where(same_bin, final[k], 0.0))
         middle = kept.shape[0] // 2
         sums = picked_right(kept[:middle], even_ref[...]) + picked_right(
             kept[middle:], odd_ref[...]
         )
         real = jnp.where(on_diagonal & ~imag_row, sums, 0.0)
-        trace = over_blocks(jnp.sum(real, axis=0, keepdims=True), group // 2)
-        part[g] = jnp.where(on_diagonal & imag_row, trace, sums)
+        trace = over_blocks(jnp.sum(real, axis=0, keepdims=True), blocks_all)
+        part[k] = jnp.where(on_diagonal & imag_row, trace, sums)
+
+    @pl.when(my_last)
+    def _():
+        last(1)
+
+    def finish(k, g):
+        final[k] = gram[g] + jnp.where(my_last, half_product(g), 0.0)
 
     own_lines = 2 * own_rows
 
-    def part_copy(peer, there, sender, sender_space):
+    def part_copy(k, peer, there, sender, sender_space):
         return pltpu.make_async_remote_copy(
-            src_ref=part.at[peer, pl.ds(pl.multiple_of(there * own_lines, own_lines), own_lines)],
+            src_ref=part.at[k, pl.ds(there * own_lines, own_lines)],
             dst_ref=rows_in.at[sender, sender_space],
-            send_sem=part_send.at[peer, there],
+            send_sem=part_send.at[k, there],
             recv_sem=part_recv.at[sender, sender_space],
             device_id={"tm": peer, "space": there},
             device_id_type=MESH,
         )
 
-    def others(k):
-        return [lax.rem(here + j, n_space) for j in range(1 if k == 0 else 0, n_space)]
-
-    order = [far + k for k in range(deep)] + [near_peer(k) for k in range(1, deep)]
-    for peer in order:
-        folded(peer)
-        for there in others(1):
-            part_copy(peer, there, me, here).start()
-    folded(me)
-    for there in others(0):
-        part_copy(me, there, me, here).start()
-    rows_in[me, here] = part[me, pl.ds(pl.multiple_of(here * own_lines, own_lines), own_lines)]
-    for there in others(0):
-        part_copy(me, here, me, there).wait_recv()
-    for peer in order:
-        for there in others(1):
-            part_copy(me, here, peer, there).wait_recv()
+    def part_arrival(sender, sender_space):
+        return part_copy(0, sender, 0, sender, sender_space)
+
+    for k in range(deep):
+        finish(k, far + k)
+    for k in range(deep):
+        fold(k)
+    for k in range(deep):
+        finish(deep + k, near + k)
+    for k in range(deep):
+        for there in range(n_space):
+            part_copy(k, far + k, there, me, here).start()
+    for k in range(deep, n):
+        fold(k)
+    for k in range(deep):
+        for there in range(n_space):
+
+            @pl.when((near + k != me) | (here != there))
+            def _(k=k, there=there):
+                part_copy(deep + k, near + k, there, me, here).start()
+
+    own = pl.ds(pl.multiple_of(here * own_lines, own_lines), own_lines)
+    rows_in[me, here] = part[deep + me - near, own]
+    for k in range(deep):
+        for there in range(n_space):
+
+            @pl.when((near + k != me) | (here != there))
+            def _(k=k, there=there):
+                part_arrival(near + k, there).wait_recv()
+
+    for k in range(deep):
+        for there in range(n_space):
+            part_arrival(far + k, there).wait_recv()
     total = rows_in[0, 0]
     for p in range(n):
         for q in range(n_space):
             if p + q > 0:
                 total = total + rows_in[p, q]
     line = lax.broadcasted_iota(jnp.int32, total.shape, 0)
-    block = lax.broadcasted_iota(jnp.int32, total.shape, 1) // (group // 2)
+    block = lax.broadcasted_iota(jnp.int32, total.shape, 1) & (blocks_all - 1)
     first = (line == own_rows) & (block == here * own_rows)
     held = jnp.sum(jnp.where(first, total, 0.0), axis=0, keepdims=True)
-    energy = over_blocks(held, group // 2)
+    energy = over_blocks(held, blocks_all)
     zero = (line >= own_rows) & (block == here * own_rows + (line & (own_rows - 1)))
-    out_ref[...] = jnp.where(zero, 0.0, total) * (blocks_all / energy)
+    spectra = jnp.where(zero, 0.0, total) * (blocks_all / energy)
+    for b in range(group // 2):
+        out_ref[b] = spectra[:, b * blocks_all : (b + 1) * blocks_all].reshape(out_ref.shape[1:])
 
     @pl.loop(0, pairs)
     def _(step):
@@ -475,11 +516,13 @@
         def _(k=k):
             half_copy(1, peer_of(k), me).wait_send()
 
-    for peer in order:
-        for there in others(1):
-            part_copy(peer, there, me, here).wait_send()
-    for there in others(0):
-        part_copy(me, there, me, here).wait_send()
+    for k in range(deep):
+        for there in range(n_space):
+            part_copy(k, far + k, there, me, here).wait_send()
+
+            @pl.when((near + k != me) | (here != there))
+            def _(k=k, there=there):
+                part_copy(deep + k, near + k, there, me, here).wait_send()
 
 
 def fused_body(snapshots, closing, weights, bin_index):
@@ -494,9 +537,9 @@
     size = blocks_all * group
     own_rows = blocks_all // n_space
     shape = (2 * own_rows, size // 2)
-    sums = pl.pallas_call(
+    return pl.pallas_call(
         functools.partial(kernel, n, n_space),
-        out_shape=jax.ShapeDtypeStruct(shape, jnp.float32),
+        out_shape=jax.ShapeDtypeStruct((group // 2, 2, own_rows, blocks_all), jnp.float32),
         in_specs=[pl.BlockSpec(memory_space=pl.ANY)] * 4,
         out_specs=pl.BlockSpec(memory_space=pltpu.VMEM),
         scratch_shapes=[
@@ -508,6 +551,7 @@
         ]
         + [pltpu.VMEM((n, size, 2 * LANES), jnp.bfloat16)] * 4
         + [
+            pltpu.VMEM((n, size, size), jnp.float32),
             pltpu.VMEM((n, size, size), jnp.float32),
             pltpu.VMEM((n, 2 * blocks_all, size // 2), jnp.float32),
             pltpu.VMEM((n, n_space) + shape, jnp.float32),
@@ -522,8 +566,6 @@
         ],
         compiler_params=pltpu.CompilerParams(collective_id=0, has_side_effects=True),
     )(snapshots, closing, weights, bin_index)
-    by_pair = sums.reshape(2, own_rows, blocks_all, group // 2)
-    return by_pair.transpose(3, 0, 1, 2)
 
 
 def chosen_body(snapshots, closing, weights, bin_index):

time: 190 us -> 188 us (0.989)
  Pallas kernels: 188 us -> 186 us
    pallas_call x1, Pallas kernels: 188 us -> 186 us  [fused_body(): pl.pallas_call(functools.partial(kernel, n, n_space), out_shape=jax.Shape...]
where the time goes in v3:
time: 188 us
  Pallas kernels  186 us (99%)
    pallas_call x1, Pallas kernels, fused_body(): pl.pallas_call(functools.partial(kernel, n, n_space), out_shape=jax.Shape...  186 us

profile of v3, /device:TPU:0, one launch (start us, length us, event | category | flops | bytes accessed | tf_op | source)
XLA Modules:
  0.0 187.9 jit_solution(3659511919232379253)
XLA Ops:
  0.0 186.5 %shard_map.46 = f32[8,2,4,16]{3,2,1,0:T(4,128)} custom-call(f32[256,7680]{1,0:T(8,128)} %snap_ref.1, f32[128,7680]{1,0:T(8,128)} %closing_ref.1, f32[7680]{0:T(1024)} %weights_ref.1, s32[64]{0:T(128)} %bins_ref.1), custom_call_target="tpu_custom_call" | custom-call | tf_op jit(solution)/shard_map/pallas_call | solution.py:540
  186.5 1.4 copy.6

commit v4 on v3

--- a/solution.py
+++ b/solution.py
@@ -539,7 +539,7 @@
     shape = (2 * own_rows, size // 2)
     return pl.pallas_call(
         functools.partial(kernel, n, n_space),
-        out_shape=jax.ShapeDtypeStruct((group // 2, 2, own_rows, blocks_all), jnp.float32),
+        out_shape=pltpu.VMEM((group // 2, 2, own_rows, blocks_all), jnp.float32),
         in_specs=[pl.BlockSpec(memory_space=pl.ANY)] * 4,
         out_specs=pl.BlockSpec(memory_space=pltpu.VMEM),
         scratch_shapes=[

time: 188 us -> 187 us (level)
  no operation moved by 1% of the time
where the time goes in v4:
time: 187 us
  Pallas kernels  186 us (99%)
    pallas_call x1, Pallas kernels, fused_body(): pl.pallas_call(functools.partial(kernel, n, n_space), out_shape=pltpu.VME...  186 us

profile of v4, /device:TPU:0, one launch (start us, length us, event | category | flops | bytes accessed | tf_op | source)
XLA Modules:
  0.0 186.5 jit_solution(4808973673989111253)
XLA Ops:
  0.0 185.9 %shard_map.46 = f32[8,2,4,16]{3,2,1,0:T(4,128)S(1)} custom-call(f32[256,7680]{1,0:T(8,128)} %snap_ref.1, f32[128,7680]{1,0:T(8,128)} %closing_ref.1, f32[7680]{0:T(1024)} %weights_ref.1, s32[64]{0:T(128)} %bins_ref.1), custom_call_target="tpu_custom_call" | custom-call | tf_op jit(solution)/shard_map/pallas_call | solution.py:540
  185.9 0.6 copy.6

commit v5 on v4

--- a/solution.py
+++ b/solution.py
@@ -293,12 +293,12 @@
 
     @pl.loop(1, pairs)
     def _(step):
-        for k in range(1, n):
+        for k in [3, 4, 5, 6, 7, 1, 2]:
             pair_copy(step, peer_of(k), me).start()
 
-    for k in range(1, n):
+    for k in [3, 4, 5, 6, 7, 1, 2]:
         half_copy(0, peer_of(k), me).start()
-    for k in range(1, n):
+    for k in [3, 4, 5, 6, 7, 1, 2]:
 
         @pl.when(has_last(peer_of(k)))
         def _(k=k):
@@ -477,8 +477,28 @@
             def _(k=k, there=there):
                 part_copy(deep + k, near + k, there, me, here).start()
 
+    @pl.loop(0, pairs)
+    def _(step):
+        for k in range(1, n):
+            pair_copy(step, peer_of(k), me).wait_send()
+
+    for k in range(1, n):
+        half_copy(0, peer_of(k), me).wait_send()
+
+        @pl.when(has_last(peer_of(k)))
+        def _(k=k):
+            half_copy(1, peer_of(k), me).wait_send()
+
     own = pl.ds(pl.multiple_of(here * own_lines, own_lines), own_lines)
     rows_in[me, here] = part[deep + me - near, own]
+    for k in range(deep):
+        for there in range(n_space):
+            part_copy(k, far + k, there, me, here).wait_send()
+
+            @pl.when((near + k != me) | (here != there))
+            def _(k=k, there=there):
+                part_copy(deep + k, near + k, there, me, here).wait_send()
+
     for k in range(deep):
         for there in range(n_space):
 
@@ -503,26 +523,6 @@
     spectra = jnp.where(zero, 0.0, total) * (blocks_all / energy)
     for b in range(group // 2):
         out_ref[b] = spectra[:, b * blocks_all : (b + 1) * blocks_all].reshape(out_ref.shape[1:])
-
-    @pl.loop(0, pairs)
-    def _(step):
-        for k in range(1, n):
-            pair_copy(step, peer_of(k), me).wait_send()
-
-    for k in range(1, n):
-        half_copy(0, peer_of(k), me).wait_send()
-
-        @pl.when(has_last(peer_of(k)))
-        def _(k=k):
-            half_copy(1, peer_of(k), me).wait_send()
-
-    for k in range(deep):
-        for there in range(n_space):
-            part_copy(k, far + k, there, me, here).wait_send()
-
-            @pl.when((near + k != me) | (here != there))
-            def _(k=k, there=there):
-                part_copy(deep + k, near + k, there, me, here).wait_send()
 
 
 def fused_body(snapshots, closing, weights, bin_index):

time: 187 us -> 186 us (level)
  no operation moved by 1% of the time
where the time goes in v5:
time: 186 us
  Pallas kernels  186 us (100%)
    pallas_call x1, Pallas kernels, fused_body(): pl.pallas_call(functools.partial(kernel, n, n_space), out_shape=pltpu.VME...  186 us

profile of v5, /device:TPU:0, one launch (start us, length us, event | category | flops | bytes accessed | tf_op | source)
XLA Modules:
  0.0 186.3 jit_solution(104032736843875925)
XLA Ops:
  0.0 185.7 %shard_map.46 = f32[8,2,4,16]{3,2,1,0:T(4,128)S(1)} custom-call(f32[256,7680]{1,0:T(8,128)} %snap_ref.1, f32[128,7680]{1,0:T(8,128)} %closing_ref.1, f32[7680]{0:T(1024)} %weights_ref.1, s32[64]{0:T(128)} %bins_ref.1), custom_call_target="tpu_custom_call" | custom-call | tf_op jit(solution)/shard_map/pallas_call | solution.py:540
  185.7 0.6 copy.6

commit v6 on v5

--- a/solution.py
+++ b/solution.py
@@ -219,10 +219,13 @@
             device_id_type=MESH,
         )
 
-    def half_copy(half, peer, sender):
+    def half_copy(half, peer, sender, cut=0, cuts=1):
+        size = rows // cuts
+        first = pl.multiple_of(sender * rows + cut * size, size)
+        source = columns(begin(peer) + 2 * pairs + half, 1)
         return pltpu.make_async_remote_copy(
-            src_ref=snap_ref.at[:, columns(begin(peer) + 2 * pairs + half, 1)],
-            dst_ref=series.at[pairs, rows_of(sender), pl.ds(half * LANES, LANES)],
+            src_ref=snap_ref.at[pl.ds(cut * size, size), source],
+            dst_ref=series.at[pairs, pl.ds(first, size), pl.ds(half * LANES, LANES)],
             send_sem=send_sem.at[pairs + half, peer],
             recv_sem=recv_sem.at[pairs + half, sender],
             device_id={"tm": peer},
@@ -298,11 +301,12 @@
 
     for k in [3, 4, 5, 6, 7, 1, 2]:
         half_copy(0, peer_of(k), me).start()
-    for k in [3, 4, 5, 6, 7, 1, 2]:
-
-        @pl.when(has_last(peer_of(k)))
-        def _(k=k):
-            half_copy(1, peer_of(k), me).start()
+    for cut in range(4):
+        for k in [3, 4, 5, 6, 7, 1, 2]:
+
+            @pl.when(has_last(peer_of(k)))
+            def _(k=k, cut=cut):
+                half_copy(1, peer_of(k), me, cut, 4).start()
 
     @pl.loop(0, pairs)
     def _(step):

time: 186 us -> 186 us (level)
  no operation moved by 1% of the time
where the time goes in v6:
time: 186 us
  Pallas kernels  186 us (100%)
    pallas_call x1, Pallas kernels, fused_body(): pl.pallas_call(functools.partial(kernel, n, n_space), out_shape=pltpu.VME...  186 us

profile of v6, /device:TPU:0, one launch (start us, length us, event | category | flops | bytes accessed | tf_op | source)
XLA Modules:
  0.0 186.3 jit_solution(14344178911992004001)
XLA Ops:
  0.0 185.7 %shard_map.46 = f32[8,2,4,16]{3,2,1,0:T(4,128)S(1)} custom-call(f32[256,7680]{1,0:T(8,128)} %snap_ref.1, f32[128,7680]{1,0:T(8,128)} %closing_ref.1, f32[7680]{0:T(1024)} %weights_ref.1, s32[64]{0:T(128)} %bins_ref.1), custom_call_target="tpu_custom_call" | custom-call | tf_op jit(solution)/shard_map/pallas_call | solution.py:544
  185.7 0.6 copy.6
